TPU v7x, 256 devices: a whole 4x4x8 slice. The times are simulated.
256 devices in a mesh: dp: 32 (over y, z), mp: 8 (over x, core).
Axes of the slice: x: 4, y: 4, z: 8, core: 2. Of those that a mesh axis runs over, the one named last changes fastest.
Arguments:
- inputs: bfloat16 [12288, 4608], P('dp', 'mp'), may hold values from -80 to 80
- queries: bfloat16 [12288, 4096], P('dp', 'mp'), may hold values from -7.5 to 7.5
- keys: bfloat16 [12288, 2048], P('dp', 'mp'), may hold values from -7.5 to 7.5
- values: bfloat16 [12288, 2048], P('dp', 'mp'), may hold values from -6 to 6
- out_weight: bfloat16 [4096, 4608], P('mp'), may hold values from -0.5 to 0.5
- norm_gain: bfloat16 [4608], P('mp'), may hold values from 0.5 to 1.5
- languages: int32 [32, 1], replicated, may hold values from 0 to 7
- lengths: int32 [32], replicated, may hold values from 193 to 384, as said below
- pattern: int32 [32, 3, 3], P('dp'), may hold values from 0 to 1, as said below
Outputs:
- counts: int32 [8], replicated
- mean: float32 [8, 4608], P(None, 'dp')
- co_moment: float32 [8, 4608, 4608], P(None, 'dp', 'mp')
Inputs may be any that keep to these rules, and one draw needn't show every extreme that they name: Each of the 8 languages is the language of one or more sequences. `lengths`: one or more sequences have all 384 tokens live. `pattern`: for each sequence there is a window w of 1 to 3 blocks such that block (q, k) is 1 exactly when q - w < k <= q.
All inputs are finite; a program needn't handle non-finite values.
Results may differ from a plain program's by a relative error of at most 0.01.
Values may be sent and summed in bfloat16 or wider, within the bound.
No kernel may reach another device: no remote copies, remote signals or barrier semaphores. Data moves between devices by JAX's collectives and lax.ppermute only.
A program may use at most 128 MiB of HBM per device.

v0:
```python
import jax
import jax.numpy as jnp
from jax import lax
from jax.sharding import PartitionSpec as P

D = 4608
H = 32
KVH = 16
HD = 128
LANGS = 8
BLK = 128
query_scale = 1.0 / 12.0
softcap = 50.0
epsilon = 1e-06


def visible(blocks, seq_len):
    spread = jnp.repeat(jnp.repeat(blocks, BLK, 0), BLK, 1)
    position = jnp.arange(seq_len)
    return (spread == 1) & (position[None, :] <= position[:, None])


def attend(queries, keys, values, blocks):
    seq_len = queries.shape[0]
    kv_local = keys.shape[1] // HD
    grouped = queries.reshape(seq_len, kv_local, H // KVH, HD)
    keyed = keys.reshape(seq_len, kv_local, HD)
    valued = values.reshape(seq_len, kv_local, HD)
    scores = (
        jnp.einsum("qkgd,tkd->kgqt", grouped, keyed, preferred_element_type=jnp.float32)
        * query_scale
    )
    capped = softcap * jnp.tanh(scores / softcap)
    allowed = visible(blocks, seq_len)
    expo = jnp.where(allowed, jnp.exp(capped), 0.0)
    weights = (expo / jnp.sum(expo, -1, keepdims=True)).astype(jnp.bfloat16)
    mixed = jnp.einsum("kgqt,tkd->qkgd", weights, valued, preferred_element_type=jnp.float32)
    return mixed.astype(jnp.bfloat16).reshape(seq_len, kv_local * (H // KVH) * HD)


def shards(inputs, queries, keys, values, out_weight, norm_gain, languages, lengths, pattern):
    seq_len = queries.shape[0]
    panel = inputs.shape[1]
    data_count = lax.axis_size("dp")
    row_width = D // data_count
    mixed = attend(queries, keys, values, pattern[0])
    output = (
        lax.psum_scatter(
            lax.dot_general(
                out_weight, mixed, (((0,), (1,)), ((), ())), preferred_element_type=jnp.float32
            ).astype(jnp.bfloat16),
            "mp",
            scatter_dimension=0,
            tiled=True,
        )
        .astype(jnp.float32)
        .T
    )
    hidden = inputs.astype(jnp.float32) + output
    square = lax.psum(jnp.sum(hidden * hidden, 1), "mp")
    normed = (
        hidden * lax.rsqrt(square[:, None] / D + epsilon) * norm_gain.astype(jnp.float32)[None, :]
    ).astype(jnp.bfloat16)
    full_rows = lax.all_gather(normed, "mp", axis=1, tiled=True)
    block_rows = lax.all_to_all(
        full_rows.reshape(seq_len, data_count, row_width),
        "dp",
        split_axis=1,
        concat_axis=0,
        tiled=True,
    ).reshape(data_count * seq_len, row_width)
    language = languages[:, 0]
    alive = (jnp.arange(seq_len)[None, :] < lengths[:, None]).astype(jnp.bfloat16)
    alive_flat = alive.reshape(-1)
    masked_rows = block_rows * alive_flat[:, None]
    onehot = language[:, None] == jnp.arange(LANGS)[None, :]
    token_weights = (onehot.astype(jnp.bfloat16)[:, None, :] * alive[:, :, None]).reshape(-1, LANGS)
    row_sums = lax.dot_general(
        token_weights, block_rows, (((0,), (0,)), ((), ())), preferred_element_type=jnp.float32
    )
    counts = jnp.sum(onehot.astype(jnp.int32) * lengths[:, None], 0)
    start_state = (
        jnp.zeros((LANGS, row_width, panel), jnp.float32),
        jnp.zeros((LANGS, panel), jnp.float32),
    )
    piece = lax.all_gather(normed, "dp", axis=0, tiled=True)
    piece_length = piece.shape[0]
    piece_span = min(piece_length, seq_len)
    turn_count = max(1, piece_length // seq_len)

    def one_sequence(turn, state):
        products, panel_sums = state
        offset = turn * piece_span
        piece_part = lax.dynamic_slice_in_dim(piece, offset, piece_span, 0)
        left_rows = lax.dynamic_slice_in_dim(masked_rows, offset, piece_span, 0)
        live_part = lax.dynamic_slice_in_dim(alive_flat, offset, piece_span, 0)
        which = lax.dynamic_index_in_dim(language, offset // seq_len, 0, False)
        term = lax.dot_general(
            left_rows, piece_part, (((0,), (0,)), ((), ())), preferred_element_type=jnp.float32
        )
        products = lax.dynamic_update_index_in_dim(
            products, lax.dynamic_index_in_dim(products, which, 0, False) + term, which, 0
        )
        panel_add = jnp.dot(live_part, piece_part, preferred_element_type=jnp.float32)
        panel_sums = lax.dynamic_update_index_in_dim(
            panel_sums, lax.dynamic_index_in_dim(panel_sums, which, 0, False) + panel_add, which, 0
        )
        return (products, panel_sums)

    products, panel_sums = lax.fori_loop(0, turn_count, one_sequence, start_state)
    scale = counts.astype(jnp.float32)
    mean = row_sums / scale[:, None]
    co_moment = (
        products - row_sums[:, :, None] * panel_sums[:, None, :] / scale[:, None, None]
    ) / scale[:, None, None]
    return (counts, mean, co_moment)


def solution(mesh):
    in_specs = (
        P("dp", "mp"),
        P("dp", "mp"),
        P("dp", "mp"),
        P("dp", "mp"),
        P("mp", None),
        P("mp"),
        P(),
        P(),
        P("dp", None, None),
    )
    out_specs = (P(), P(None, "dp"), P(None, "dp", "mp"))
    return jax.shard_map(shards, mesh=mesh, in_specs=in_specs, out_specs=out_specs, check_vma=False)
```

profile of v0, /device:TPU:1, one launch (start us, length us, event | category | flops | bytes accessed | tf_op | source)
XLA Modules:
  0.0 477.5 jit_solution(18366444567374238282)
XLA Ops:
  13.4 4.5 fusion.7
  17.9 3.6 copy.71
  22.8 39.3 %reduce-scatter.4.cloned.1.call-done = bf16[576,384]{1,0:T(8,128)(2,1)} async-done(((bf16[4608,384]{1,0:T(8,128)(2,1)}), bf16[576,384]{1,0:T(8,128)(2,1)}) %reduce-scatter.4.cloned.1.call-update) | async-done | bytes 442384
  62.2 1.3 copy.72
  63.7 15.0 %psum.7 = f32[384]{0:T(512)S(1)} all-reduce(f32[384]{0:T(512)S(1)} %multiply_reduce_fusion), channel_id=1, replica_groups=mesh['dp'=32,'mp'=8] {'mp'}, use_global_device_ids=true, to_apply=%region_4.5 | all-reduce | flops 384 | bytes 3072 | tf_op jit(solution)/shard_map/psum | solution.py:60
  80.6 31.0 %all-gather.3.cloned.1.call-done = bf16[384,4608]{0,1:T(8,128)(2,1)} async-done(((bf16[384,576]{0,1:T(8,128)(2,1)}), bf16[384,4608]{0,1:T(8,128)(2,1)}) %all-gather.3.cloned.1.call-update) | async-done | bytes 3538960 | tf_op jit(solution)/shard_map/all_gather | solution.py:64
  111.6 9.7 %all-to-all-start = ((bf16[384,32,144]{0,2,1:T(8,128)(2,1)}), bf16[384,32,144]{0,2,1:T(8,128)(2,1)S(1)}, u32[]{:S(2)}, u32[]{:S(2)}) async-start(bf16[384,32,144]{0,2,1:T(8,128)(2,1)} %bitcast.68), calls=%async_computation | async-start | bytes 7077888 | tf_op jit(solution)/shard_map/all_to_all | solution.py:65
  122.1 1.3 fusion.12
  123.4 1.4 reshape.147
  124.8 1.5 broadcast_multiply_fusion.1
  126.3 92.5 %all-to-all-done = bf16[384,32,144]{0,2,1:T(8,128)(2,1)S(1)} async-done(((bf16[384,32,144]{0,2,1:T(8,128)(2,1)}), bf16[384,32,144]{0,2,1:T(8,128)(2,1)S(1)}, u32[]{:S(2)}, u32[]{:S(2)}) %all-to-all-start) | async-done | bytes 3538976 | tf_op jit(solution)/shard_map/all_to_all | solution.py:65
  219.8 1.6 broadcast_divide_fusion
  221.4 2.0 broadcast_multiply_fusion
  223.4 70.8 %all-gather.5.cloned.1.call-done = bf16[12288,576]{1,0:T(8,128)(2,1)} async-done(((bf16[384,576]{1,0:T(8,128)(2,1)}), bf16[12288,576]{1,0:T(8,128)(2,1)}) %all-gather.5.cloned.1.call-update) | async-done | bytes 14155792 | tf_op jit(solution)/shard_map/all_gather | solution.py:86
  294.5 174.3 %while.17 = (s32[]{:T(128)}, f32[8,144,576]{2,1,0:T(8,128)S(1)}, f32[8,576]{1,0:T(8,128)S(1)}, s32[32]{0:T(128)S(1)}, bf16[12288,144]{0,1:T(8,128)(2,1)}, /*inde...) while((s32[]{:T(128)}, f32[8,144,576]{2,1,0:T(8,128)S(1)}, ...), condition=%wide.region_6.7_spmd, body=%wide.region_5.6_spmd.sunk | while | flops 64226900 | bytes 2523245 | solution.py:110
  297.1 1.4 fusion.31
  302.5 1.4 fusion.31
  308.0 1.4 fusion.31
  313.4 1.4 fusion.31
  318.9 1.4 fusion.31
  324.3 1.4 fusion.31
  329.8 1.4 fusion.31
  335.2 1.4 fusion.31
  340.7 1.4 fusion.31
  346.1 1.4 fusion.31
  351.6 1.4 fusion.31
  357.0 1.4 fusion.31
  362.5 1.4 fusion.31
  367.9 1.4 fusion.31
  373.4 1.4 fusion.31
  378.8 1.4 fusion.31
  384.2 1.4 fusion.31
  389.7 1.4 fusion.31
  395.1 1.4 fusion.31
  400.6 1.4 fusion.31
  406.0 1.4 fusion.31
  411.5 1.4 fusion.31
  416.9 1.4 fusion.31
  422.4 1.4 fusion.31
  427.8 1.4 fusion.31
  433.3 1.4 fusion.31
  438.7 1.4 fusion.31
  444.2 1.4 fusion.31
  449.6 1.4 fusion.31
  455.1 1.4 fusion.31
  460.5 1.4 fusion.31
  466.0 1.4 fusion.31
  468.8 2.1 subtract_divide_fusion
  (335 shorter events, 76.4 us)
Async XLA Ops:
  7.2 55.0 %reduce-scatter.4.cloned.1.call-start = ((), (), s32[]{:S(2)}) async-start(), calls=%async_computation.4 | async-start | bytes 3981312
  21.5 1.0 copy-start.2
  21.5 1.3 copy-start.4
  21.6 90.1 %all-gather.3.cloned.1.call-start = ((), (), s32[]{:S(2)}) async-start(), calls=%async_computation.2 | async-start | bytes 3981312 | tf_op jit(solution)/shard_map/all_gather | solution.py:64
  78.9 1.0 copy-start
  79.9 214.4 %all-gather.5.cloned.1.call-start = ((), (), s32[]{:S(2)}) async-start(), calls=%async_computation.3 | async-start | bytes 16220160 | tf_op jit(solution)/shard_map/all_gather | solution.py:86
  111.6 9.7 %copy-start.5 = (s32[32]{0:T(128)S(1)}, s32[32]{0:T(128)}, u32[]{:S(2)}) copy-start(s32[32]{0:T(128)} %param.18) | copy-start | bytes 388
  111.6 9.7 %copy-start.6 = (s32[32,1]{0,1:T(1,128)S(1)}, s32[32,1]{0,1:T(1,128)}, u32[]{:S(2)}) copy-start(s32[32,1]{0,1:T(1,128)} %param.17) | copy-start | bytes 388
  111.6 107.2 %all-to-all-start = ((bf16[384,32,144]{0,2,1:T(8,128)(2,1)}), bf16[384,32,144]{0,2,1:T(8,128)(2,1)S(1)}, u32[]{:S(2)}, u32[]{:S(2)}) async-start(bf16[384,32,144]{0,2,1:T(8,128)(2,1)} %bitcast.68), calls=%async_computation | async-start | bytes 7077888 | tf_op jit(solution)/shard_map/all_to_all | solution.py:65
  121.5 0.5 copy-start.8
  218.9 0.9 copy-start.1
  219.4 2.0 copy-start.3
  223.4 71.0 %copy-start.7 = (s32[32,1]{0,1:T(1,128)S(1)}, s32[32,1]{0,1:T(1,128)}, u32[]{:S(2)}) copy-start(s32[32,1]{0,1:T(1,128)} %param.17) | copy-start | bytes 388
Sparse Core Ops, SparseCore 0:
  21.7 40.4 reduce-scatter.3
  80.0 31.5 all-gather.2
  114.8 179.3 all-gather.4
where the time goes:
time: 481 us; the launch traced here: 477 us
  waiting for transfers between devices  234 us (49%)
  matrix products  91 us (19%)
  loops' own time  65.3 us (14%)
  local copies, waits for them, and re-layouts  39.5 us (8%)
  blocking collectives  15 us (3%)
  between operations  13.9 us (3%)
  starting transfers between devices  9.82 us (2%)
  other arithmetic  8.46 us (2%)
    all_to_all x1, waiting for transfers between devices, shards(): lax.all_to_all(full_rows.reshape(seq_len, data_count, row_width), 'dp', s...  92.5 us
    all_gather x1, waiting for transfers between devices, shards(): piece = lax.all_gather(normed, 'dp', axis=0, tiled=True)  70.8 us
    another operation x1, loops' own time, shards(): lax.fori_loop(0, turn_count, one_sequence, start_state)  65.3 us
    dot_general x32, matrix products, one_sequence(): lax.dot_general(left_rows, piece_part, (((0,), (0,)), ((), ())), preferre...  44.1 us
    unnamed x4, waiting for transfers between devices  40 us
    dot_general x32, matrix products, one_sequence(): jnp.dot(live_part, piece_part, preferred_element_type=jnp.float32)  38.8 us
    all_gather x1, waiting for transfers between devices, shards(): full_rows = lax.all_gather(normed, 'mp', axis=1, tiled=True)  31 us
    dynamic_slice x32, local copies, waits for them, and re-layouts, one_sequence(): which = lax.dynamic_index_in_dim(language, offset // seq_len, 0, False)  18.8 us
  transfers between devices with their start and end apart: 4, of which 4 were waited for; matrix products, arithmetic and copies ran while one was open for 2% of the time, Pallas kernels for 0%

commit v1 on v0

--- a/solution.py
+++ b/solution.py
@@ -62,12 +62,18 @@
         hidden * lax.rsqrt(square[:, None] / D + epsilon) * norm_gain.astype(jnp.float32)[None, :]
     ).astype(jnp.bfloat16)
     full_rows = lax.all_gather(normed, "mp", axis=1, tiled=True)
-    block_rows = lax.all_to_all(
-        full_rows.reshape(seq_len, data_count, row_width),
-        "dp",
-        split_axis=1,
-        concat_axis=0,
-        tiled=True,
+    block_rows = jnp.concatenate(
+        lax.all_to_all(
+            jnp.stack(
+                jnp.split(
+                    full_rows.reshape(seq_len, data_count, row_width), lax.axis_size("dp"), axis=1
+                )
+            ),
+            "dp",
+            0,
+            0,
+        ),
+        axis=0,
     ).reshape(data_count * seq_len, row_width)
     language = languages[:, 0]
     alive = (jnp.arange(seq_len)[None, :] < lengths[:, None]).astype(jnp.bfloat16)

time: 481 us -> 498 us (1.035)
  local copies, waits for them, and re-layouts: 39.5 us -> 74.9 us
  waiting for transfers between devices: 234 us -> 216 us
    unnamed x24 -> x57, local copies, waits for them, and re-layouts: 7.59 us -> 42.3 us
    all_gather x1, waiting for transfers between devices: 70.8 us -> 39.3 us  [shards(): piece = lax.all_gather(normed, 'dp', axis=0, tiled=True)]
    all_to_all x1, waiting for transfers between devices: 92.5 us -> 105 us  [shards(): lax.all_to_all(jnp.stack(jnp.split(full_rows.reshape(seq_len, data_count,...]
  transfers between devices with their start and end apart: 4 -> 4, of which waited for: 4 -> 4; matrix products, arithmetic and copies ran while one was open for 2% -> 9% of each run, Pallas kernels for 0% -> 0%
where the time goes in v1:
time: 498 us; the launch traced here: 494 us
  waiting for transfers between devices  216 us (43%)
  matrix products  91 us (18%)
  local copies, waits for them, and re-layouts  74.9 us (15%)
  loops' own time  65.3 us (13%)
  blocking collectives  15 us (3%)
  between operations  13.9 us (3%)
  starting transfers between devices  9.82 us (2%)
  other arithmetic  8.44 us (2%)
    all_to_all x1, waiting for transfers between devices, shards(): lax.all_to_all(jnp.stack(jnp.split(full_rows.reshape(seq_len, data_count,...  105 us
    another operation x1, loops' own time, shards(): lax.fori_loop(0, turn_count, one_sequence, start_state)  65.3 us
    dot_general x32, matrix products, one_sequence(): lax.dot_general(left_rows, piece_part, (((0,), (0,)), ((), ())), preferre...  44 us
    unnamed x57, local copies, waits for them, and re-layouts  42.3 us
    unnamed x4, waiting for transfers between devices  40 us
    all_gather x1, waiting for transfers between devices, shards(): piece = lax.all_gather(normed, 'dp', axis=0, tiled=True)  39.3 us
    dot_general x32, matrix products, one_sequence(): jnp.dot(live_part, piece_part, preferred_element_type=jnp.float32)  38.8 us
    all_gather x1, waiting for transfers between devices, shards(): full_rows = lax.all_gather(normed, 'mp', axis=1, tiled=True)  31 us
  transfers between devices with their start and end apart: 4, of which 4 were waited for; matrix products, arithmetic and copies ran while one was open for 9% of the time, Pallas kernels for 0%

profile of v1, /device:TPU:1, one launch (start us, length us, event | category | flops | bytes accessed | tf_op | source)
XLA Modules:
  0.0 494.0 jit_solution(6878994738741618268)
XLA Ops:
  13.4 4.5 fusion.7
  17.9 3.6 copy.101
  22.8 39.3 %reduce-scatter.4.cloned.1.call-done = bf16[576,384]{1,0:T(8,128)(2,1)} async-done(((bf16[4608,384]{1,0:T(8,128)(2,1)}), bf16[576,384]{1,0:T(8,128)(2,1)}) %reduce-scatter.4.cloned.1.call-update) | async-done | bytes 442384
  63.7 15.0 %psum.7 = f32[384]{0:T(512)S(1)} all-reduce(f32[384]{0:T(512)S(1)} %multiply_reduce_fusion), channel_id=1, replica_groups=mesh['dp'=32,'mp'=8] {'mp'}, use_global_device_ids=true, to_apply=%region_4.5 | all-reduce | flops 384 | bytes 3072 | tf_op jit(solution)/shard_map/psum | solution.py:60
  80.6 31.0 %all-gather.3.cloned.1.call-done = bf16[384,4608]{0,1:T(8,128)(2,1)} async-done(((bf16[384,576]{0,1:T(8,128)(2,1)}), bf16[384,4608]{0,1:T(8,128)(2,1)}) %all-gather.3.cloned.1.call-update) | async-done | bytes 3538960 | tf_op jit(solution)/shard_map/all_gather | solution.py:64
  111.6 1.7 fusion.43
  113.3 1.5 fusion.42
  114.9 1.5 fusion.41
  116.4 1.5 fusion.40
  118.0 1.5 fusion.39
  119.5 1.5 fusion.38
  121.0 1.5 fusion.37
  122.6 1.6 fusion.36
  124.1 1.6 fusion.35
  125.7 1.6 fusion.34
  127.3 1.6 fusion.33
  128.8 1.5 fusion.32
  130.4 1.6 fusion.31
  131.9 1.5 fusion.30
  133.5 1.6 fusion.29
  135.0 1.5 fusion.28
  147.1 9.7 %all-to-all-start = ((bf16[32,384,1,144]{1,3,2,0:T(8,128)(2,1)}), bf16[32,384,1,144]{1,3,2,0:T(8,128)(2,1)S(1)}, u32[]{:S(2)}, u32[]{:S(2)}) async-start(bf16[32,384,1,144]{1,3,2,0:T(8,128)(2,1)} %fusion.12), calls=%async_computation | async-start | bytes 7077888 | tf_op jit(solution)/shard_map/all_to_all | solution.py:66
  160.2 1.5 broadcast_multiply_fusion.1
  161.7 105.2 %all-to-all-done = bf16[32,384,1,144]{1,3,2,0:T(8,128)(2,1)S(1)} async-done(((bf16[32,384,1,144]{1,3,2,0:T(8,128)(2,1)}), bf16[32,384,1,144]{1,3,2,0:T(8,128)(2,1)S(1)}, u32[]{:S(2)}, u32[]{:S(2)}) %all-to-all-start) | async-done | bytes 3538976 | tf_op jit(solution)/shard_map/all_to_all | solution.py:66
  267.9 1.6 broadcast_divide_fusion
  269.5 2.0 broadcast_multiply_fusion
  271.5 39.3 %all-gather.5.cloned.1.call-done = bf16[12288,576]{1,0:T(8,128)(2,1)} async-done(((bf16[384,576]{1,0:T(8,128)(2,1)}), bf16[12288,576]{1,0:T(8,128)(2,1)}) %all-gather.5.cloned.1.call-update) | async-done | bytes 14155792 | tf_op jit(solution)/shard_map/all_gather | solution.py:92
  311.0 174.4 %while.17 = (s32[]{:T(128)}, f32[8,144,576]{2,1,0:T(8,128)S(1)}, f32[8,576]{1,0:T(8,128)S(1)}, s32[32]{0:T(128)S(1)}, bf16[12288,144]{0,1:T(8,128)(2,1)}, /*inde...) while((s32[]{:T(128)}, f32[8,144,576]{2,1,0:T(8,128)S(1)}, ...), condition=%wide.region_6.7_spmd, body=%wide.region_5.6_spmd.sunk | while | flops 64226900 | bytes 2523245 | solution.py:116
  313.6 1.4 fusion.63
  335.4 1.4 fusion.63
  340.9 1.4 fusion.63
  346.3 1.4 fusion.63
  351.8 1.4 fusion.63
  357.2 1.4 fusion.63
  362.7 1.4 fusion.63
  368.1 1.4 fusion.63
  373.6 1.4 fusion.63
  379.0 1.4 fusion.63
  389.9 1.4 fusion.63
  395.4 1.4 fusion.63
  400.8 1.4 fusion.63
  406.3 1.4 fusion.63
  411.7 1.4 fusion.63
  417.2 1.4 fusion.63
  422.6 1.4 fusion.63
  428.1 1.4 fusion.63
  433.5 1.4 fusion.63
  485.4 2.1 subtract_divide_fusion
  (369 shorter events, 108.8 us)
Async XLA Ops:
  7.2 55.0 %reduce-scatter.4.cloned.1.call-start = ((), (), s32[]{:S(2)}) async-start(), calls=%async_computation.4 | async-start | bytes 3981312
  21.5 1.0 copy-start.3
  21.5 1.3 copy-start.5
  21.6 90.1 %all-gather.3.cloned.1.call-start = ((), (), s32[]{:S(2)}) async-start(), calls=%async_computation.2 | async-start | bytes 3981312 | tf_op jit(solution)/shard_map/all_gather | solution.py:64
  78.9 1.0 copy-start
  79.9 230.9 %all-gather.5.cloned.1.call-start = ((), (), s32[]{:S(2)}) async-start(), calls=%async_computation.3 | async-start | bytes 16220160 | tf_op jit(solution)/shard_map/all_gather | solution.py:92
  111.6 25.0 %copy-start.1 = (bf16[384,4608]{0,1:T(8,128)(2,1)S(1)}, bf16[384,4608]{0,1:T(8,128)(2,1)}, u32[]{:S(2)}) copy-start(bf16[384,4608]{0,1:T(8,128)(2,1)} %all-gather.3.cloned.1.call-done) | copy-start | bytes 10616836
  147.1 9.7 %copy-start.6 = (s32[32]{0:T(128)S(1)}, s32[32]{0:T(128)}, u32[]{:S(2)}) copy-start(s32[32]{0:T(128)} %param.18) | copy-start | bytes 388
  147.1 9.7 %copy-start.7 = (s32[32,1]{0,1:T(1,128)S(1)}, s32[32,1]{0,1:T(1,128)}, u32[]{:S(2)}) copy-start(s32[32,1]{0,1:T(1,128)} %param.17) | copy-start | bytes 388
  147.1 119.9 %all-to-all-start = ((bf16[32,384,1,144]{1,3,2,0:T(8,128)(2,1)}), bf16[32,384,1,144]{1,3,2,0:T(8,128)(2,1)S(1)}, u32[]{:S(2)}, u32[]{:S(2)}) async-start(bf16[32,384,1,144]{1,3,2,0:T(8,128)(2,1)} %fusion.12), calls=%async_computation | async-start | bytes 7077888 | tf_op jit(solution)/shard_map/all_to_all | solution.py:66
  156.9 0.5 copy-start.9
  266.9 0.9 copy-start.2
  267.5 2.0 copy-start.4
  269.5 41.5 %copy-start.8 = (s32[32,1]{0,1:T(1,128)S(1)}, s32[32,1]{0,1:T(1,128)}, u32[]{:S(2)}) copy-start(s32[32,1]{0,1:T(1,128)} %param.17) | copy-start | bytes 388
Sparse Core Ops, SparseCore 0:
  21.7 40.4 reduce-scatter.3
  80.0 31.5 all-gather.2
  114.8 195.9 all-gather.4
